TPU v7x, 32 devices: a whole 2x2x4 slice. The times are simulated.
32 devices in a mesh: ch: 4 (over y, x), row: 8 (over z, core).
Axes of the slice: x: 2, y: 2, z: 4, core: 2. Of those that a mesh axis runs over, the one named last changes fastest.
Arguments:
- latent: bfloat16 [128, 32, 1280], P('row', None, 'ch'), may hold values from -50 to 50
- timestep: int32 [4], replicated, may hold values from 0 to 999
- norm_gain_a: float32 [1280], P('ch'), may hold values from 0.1 to 1.9
- conv_weight_a: bfloat16 [1280, 3, 3, 1280], P('ch'), may hold values from -0.0546875 to 0.0546875
- time_weight: bfloat16 [320, 1280], P(None, 'ch'), may hold values from -0.3125 to 0.3125
- norm_gain_b: float32 [1280], P('ch'), may hold values from 0.1 to 1.9
- conv_weight_b: bfloat16 [1280, 3, 3, 1280], P('ch'), may hold values from -0.0546875 to 0.0546875
- norm_gain_c: float32 [1280], P('ch'), may hold values from 0.1 to 1.9
- w_query: bfloat16 [1024, 1280], P('ch'), may hold values from -4 to 4
- w_key: bfloat16 [1024, 1280], P('ch'), may hold values from -4 to 4
- w_value: bfloat16 [1024, 1280], P('ch'), may hold values from -0.3125 to 0.3125
- w_out: bfloat16 [1280, 1024], P('ch'), may hold values from -0.1875 to 0.1875
Outputs:
- result: bfloat16 [128, 32, 1280], P('row', None, 'ch')
All inputs are finite; a program needn't handle non-finite values.
Results may differ from a plain program's by a relative error of at most 0.017.
Values may be sent and summed in bfloat16 or wider, within the bound.
A program may use at most 64 MiB of HBM per device.

v0:
```python
import math
import jax
import jax.numpy as jnp
from jax import lax
from jax.sharding import PartitionSpec as P

C = 1280
GROUPS = 32
HEAD_DIM = 64
TDIM = 320
H = 32
eps_value = 1e-06


def swapped(value, axis, stride):
    mask = 2**stride
    pairs = [(source, source ^ mask) for source in range(lax.axis_size(axis))]
    return lax.ppermute(value, axis, pairs)


def right_product(left, weight):
    return lax.dot_general(
        left, weight, (((1,), (1,)), ((), ())), preferred_element_type=jnp.float32
    )


def conv_taps(padded, weight):
    outcome = lax.conv_general_dilated(
        padded[None],
        weight,
        (1, 1),
        "VALID",
        dimension_numbers=("NHWC", "OHWI", "NHWC"),
        preferred_element_type=jnp.float32,
    )
    return outcome[0]


def pad_columns(field):
    return jnp.pad(field, ((0, 0), (1, 1), (0, 0)))


def body(
    latent,
    timestep,
    norm_gain_a,
    conv_weight_a,
    time_weight,
    norm_gain_b,
    conv_weight_b,
    norm_gain_c,
    w_query,
    w_key,
    w_value,
    w_out,
):
    rows, width, local_ch = latent.shape
    span = H // rows
    place = lax.axis_index("row")
    within = place % span
    image_id = place // span
    group_width = C // GROUPS
    local_groups = local_ch // group_width
    members = float(H * width * group_width)
    tokens = rows * width

    def group_norm(value, gain):
        flat = value.reshape(tokens, local_groups, group_width)
        stats = jnp.stack([jnp.sum(flat, axis=(0, 2)), jnp.sum(flat * flat, axis=(0, 2))])
        stats = stats + swapped(stats, "row", 0)
        mean = stats[0] / members
        spread = stats[1] / members - mean * mean
        scaled = (flat - mean[None, :, None]) * lax.rsqrt(spread + eps_value)[None, :, None]
        return scaled.reshape(rows, width, local_ch) * gain

    upper_half = within == 0

    def facing_row(field):
        return jnp.where(upper_half, field[-1:], field[:1])

    def attach_rim(field, partner):
        empty_row = jnp.zeros_like(partner)
        above = jnp.where(upper_half, empty_row, partner)
        below = jnp.where(upper_half, partner, empty_row)
        return jnp.concatenate([above, field, below], axis=0)

    def convolve(active, weight):
        full = lax.all_gather(active, "ch", axis=2, tiled=True)
        partner = swapped(facing_row(full), "row", 0)
        rimmed = attach_rim(full, partner)
        result_conv = conv_taps(pad_columns(rimmed), weight)
        return result_conv

    image_ids = jnp.arange(timestep.shape[0])
    step_value = jnp.sum(jnp.where(image_ids == image_id, timestep, 0)).astype(jnp.float32)
    half = TDIM // 2
    freqs = jnp.exp(-math.log(10000.0) * jnp.arange(half, dtype=jnp.float32) / half)
    angles = step_value * freqs
    sinus = jnp.concatenate([jnp.cos(angles), jnp.sin(angles)])[None, :].astype(jnp.bfloat16)
    time_add = jax.nn.silu(jnp.dot(sinus, time_weight, preferred_element_type=jnp.float32))
    source = latent.astype(jnp.float32)
    active_a = jax.nn.silu(group_norm(source, norm_gain_a)).astype(jnp.bfloat16)
    hidden_a = convolve(active_a, conv_weight_a) + time_add[None]
    active_b = jax.nn.silu(group_norm(hidden_a, norm_gain_b)).astype(jnp.bfloat16)
    hidden_b = source + convolve(active_b, conv_weight_b)
    normed = group_norm(hidden_b, norm_gain_c).astype(jnp.bfloat16).reshape(tokens, local_ch)
    inner = w_query.shape[0]
    projections = jnp.concatenate([w_query, w_key, w_value], axis=0)
    weight_cols = projections
    mixed = right_product(lax.all_gather(normed, "ch", axis=1, tiled=True), weight_cols)
    query = mixed[:, :inner].astype(jnp.bfloat16)
    keyed = mixed[:, inner : 2 * inner].astype(jnp.bfloat16)
    valued = mixed[:, 2 * inner :].astype(jnp.bfloat16)
    key_value = jnp.stack([keyed, valued])
    key_value = jnp.concatenate([key_value, swapped(key_value, "row", 0)], axis=1)
    local_heads = inner // HEAD_DIM
    query_heads = query.reshape(tokens, local_heads, HEAD_DIM)
    key_heads = key_value[0].reshape(-1, local_heads, HEAD_DIM)
    value_heads = key_value[1].reshape(-1, local_heads, HEAD_DIM)
    scores = jnp.einsum(
        "qhd,khd->hqk", query_heads, key_heads, preferred_element_type=jnp.float32
    ) * (1.0 / math.sqrt(HEAD_DIM))
    highest = jnp.max(scores, axis=-1, keepdims=True)
    raised = jnp.exp(scores - highest)
    weights = (raised / jnp.sum(raised, axis=-1, keepdims=True)).astype(jnp.bfloat16)
    heads_out = jnp.einsum("hqk,khd->qhd", weights, value_heads, preferred_element_type=jnp.float32)
    heads_out = heads_out.astype(jnp.bfloat16).reshape(tokens, inner)
    weight_cols = w_out
    projected = right_product(lax.all_gather(heads_out, "ch", axis=1, tiled=True), weight_cols)
    total = hidden_b.reshape(tokens, local_ch) + projected
    return total.reshape(rows, width, local_ch).astype(jnp.bfloat16)


def solution(mesh):
    return jax.shard_map(
        body,
        mesh=mesh,
        in_specs=(
            P("row", None, "ch"),
            P(),
            P("ch"),
            P("ch", None, None, None),
            P(None, "ch"),
            P("ch"),
            P("ch", None, None, None),
            P("ch"),
            P("ch", None),
            P("ch", None),
            P("ch", None),
            P("ch", None),
        ),
        out_specs=P("row", None, "ch"),
        check_vma=False,
    )
```

profile of v0, /device:TPU:0, one launch (start us, length us, event | category | flops | bytes accessed | tf_op | source)
XLA Modules:
  0.0 277.8 jit_solution(7291214916432832792)
XLA Ops:
  6.5 1.3 convert_reduce_fusion
  9.9 1.3 fusion.55
  11.2 1.8 copy.96
  14.7 62.4 %all-gather.5.cloned.1.call-done = bf16[16,32,1280]{1,0,2:T(8,128)(2,1)} async-done(((bf16[16,32,320]{1,0,2:T(8,128)(2,1)}), bf16[16,32,1280]{1,0,2:T(8,128)(2,1)}) %all-gather.5.cloned.1.call-update) | async-done | bytes 1310736 | tf_op jit(solution)/shard_map/all_gather | solution.py:88
  77.1 3.0 %broadcast_select_fusion.5 = bf16[1,32,1280]{1,0,2:T(2,128)(2,1)S(1)} fusion(pred[]{:T(512)S(6)} %eq.11, bf16[16,32,1280]{1,0,2:T(8,128)(2,1)} %all-gather.5.cloned.1.call-done), kind=kLoop, calls=%fused_computation.48 | loop fusion | flops 40960 | bytes 245761 | tf_op jit(solution)/shard_map/jit(_where)/select_n | solution.py:79
  80.6 6.0 %copy.101 = bf16[16,32,1280]{2,1,0:T(8,128)(2,1)S(1)} copy(bf16[16,32,1280]{1,0,2:T(8,128)(2,1)} %all-gather.5.cloned.1.call-done) | data formatting | bytes 2621440 | tf_op jit(solution)/shard_map/all_gather | solution.py:88
  87.1 1.9 broadcast_select_fusion.4
  89.0 1.3 copy.100
  92.3 1.1 slice-done
  94.5 7.8 %select_reduce_fusion.1 = (f32[320]{0:T(512)S(1)}, f32[320]{0:T(512)S(1)}, f32[16,8,5,320]{3,1,2,0:T(8,128)S(1)}) fusion(f32[320]{0:T(512)S(1)} %divide_multiply_fusion, pred[8,5]{0,1:T(8,128)(4,1)S(1)} %copy-done.8, bf16[320,3,3,1280]{3,0,2,1:T(8,128)(2,1)S(1)} %bitcast.121, bf16[18,1,7,2,1280]{4,2,3,0,1:T(8,128)(2,1)S(1)} %slice.69, ...), kind=kOutput, calls=%fused_computation.59 | convolution fusion | flops 4727766016 | bytes 10684200 | tf_op jit(solution)/shard_map/conv_general_dilated | solution.py:28
  104.8 2.0 copy.107
  106.8 61.4 %all-gather.7.cloned.1.call-done = bf16[16,32,1280]{1,0,2:T(8,128)(2,1)} async-done(((bf16[16,32,320]{1,0,2:T(8,128)(2,1)}), bf16[16,32,1280]{1,0,2:T(8,128)(2,1)}) %all-gather.7.cloned.1.call-update) | async-done | bytes 1310736 | tf_op jit(solution)/shard_map/all_gather | solution.py:88
  168.2 3.0 %broadcast_select_fusion.2 = bf16[1,32,1280]{1,0,2:T(2,128)(2,1)S(1)} fusion(pred[]{:T(512)S(6)} %eq.11, bf16[16,32,1280]{1,0,2:T(8,128)(2,1)} %all-gather.7.cloned.1.call-done), kind=kLoop, calls=%fused_computation.45 | loop fusion | flops 40960 | bytes 245761 | tf_op jit(solution)/shard_map/jit(_where)/select_n | solution.py:79
  171.7 6.0 %copy.112 = bf16[16,32,1280]{2,1,0:T(8,128)(2,1)S(1)} copy(bf16[16,32,1280]{1,0,2:T(8,128)(2,1)} %all-gather.7.cloned.1.call-done) | data formatting | bytes 2621440 | tf_op jit(solution)/shard_map/all_gather | solution.py:88
  178.2 1.9 broadcast_select_fusion.1
  180.1 1.3 copy.111
  185.6 7.8 %fusion.35 = f32[16,8,5,320]{3,1,2,0:T(8,128)S(1)} fusion(bf16[320,3,3,1280]{3,0,2,1:T(8,128)(2,1)S(1)} %bitcast.123, bf16[18,1,7,2,1280]{4,2,3,0,1:T(8,128)(2,1)S(1)} %slice.73, bf16[18,1,8,5,1280]{4,2,3,0,1:T(8,128)(2,1)S(1)} %copy.116, pred[8,5]{0,1:T(8,128)(4,1)S(1)} %copy-done.8), kind=kOutput, calls=%fused_computation.49 | convolution fusion | flops 4726538240 | bytes 10680360 | tf_op jit(solution)/shard_map/conv_general_dilated | solution.py:28
  197.2 28.8 %all-gather.9.cloned.1.call-done = bf16[512,1280]{0,1:T(8,128)(2,1)} async-done(((bf16[512,320]{0,1:T(8,128)(2,1)}), bf16[512,1280]{0,1:T(8,128)(2,1)}) %all-gather.9.cloned.1.call-update) | async-done | bytes 1310736 | tf_op jit(solution)/shard_map/all_gather | solution.py:110
  225.9 2.7 fusion.32
  229.0 1.7 collective-permute-done.5
  231.3 5.0 %fusion.81 = (f32[4,512]{1,0:T(4,128)S(1)}, f32[4,512,1024]{2,1,0:T(8,128)}) fusion(bf16[512,4,64]{0,2,1:T(8,128)(2,1)S(1)} %bitcast.106, bf16[1024,4,64]{0,2,1:T(8,128)(2,1)S(1)} %bitcast.104), kind=kOutput, calls=%fused_computation.118 | convolution fusion | flops 274727936 | bytes 9183232 | tf_op jit(solution)/shard_map/sub | solution.py:124
  236.4 5.5 %fusion.44 = bf16[4,64,512]{2,1,0:T(8,128)(2,1)} fusion(bf16[1024,4,64]{0,2,1:T(8,128)(2,1)S(1)} %bitcast.105, f32[4,512,1024]{2,1,0:T(8,128)} %get-tuple-element.23, f32[4,512]{1,0:T(4,128)S(1)} %get-tuple-element.22), kind=kOutput, calls=%fused_computation.55 | convolution fusion | flops 272760832 | bytes 9183232 | tf_op jit(solution)/shard_map/hqk,khd->qhd/dot_general | solution.py:126
  242.5 26.1 %all-gather.11.cloned.1.call-done = bf16[512,1024]{0,1:T(8,128)(2,1)} async-done(((bf16[512,256]{0,1:T(8,128)(2,1)}), bf16[512,1024]{0,1:T(8,128)(2,1)}) %all-gather.11.cloned.1.call-update) | async-done | bytes 1048592 | tf_op jit(solution)/shard_map/all_gather | solution.py:129
  268.6 1.7 fusion.43
  (121 shorter events, 20.7 us)
Async XLA Ops:
  6.5 262.1 %copy-start = (bf16[320,1024]{1,0:T(8,128)(2,1)S(1)}, bf16[320,1024]{1,0:T(8,128)(2,1)}, u32[]{:S(2)}) copy-start(bf16[320,1024]{1,0:T(8,128)(2,1)} %param.23) | copy-start | bytes 1966084
  6.5 6.6 %copy-start.7 = (s32[4]{0:T(128)S(1)}, s32[4]{0:T(128)}, u32[]{:S(2)}) copy-start(s32[4]{0:T(128)} %param.13) | copy-start | bytes 52
  6.5 8.0 %copy-start.2 = (bf16[320,320]{1,0:T(8,128)(2,1)S(1)}, bf16[320,320]{1,0:T(8,128)(2,1)}, u32[]{:S(2)}) copy-start(bf16[320,320]{1,0:T(8,128)(2,1)} %param.16) | copy-start | bytes 614404
  6.5 70.5 %all-gather.5.cloned.1.call-start = ((), (), s32[]{:S(2)}) async-start(), calls=%async_computation | async-start | bytes 6553600 | tf_op jit(solution)/shard_map/all_gather | solution.py:88
  8.2 1.4 collective-permute-start
  13.0 155.2 %all-gather.7.cloned.1.call-start = ((), (), s32[]{:S(2)}) async-start(), calls=%async_computation.1 | async-start | bytes 6553600 | tf_op jit(solution)/shard_map/all_gather | solution.py:88
  80.5 6.1 %collective-permute-start.1 = (bf16[1,32,1280]{2,1,0:T(8,128)(2,1)S(1)}, bf16[1,32,1280]{2,1,0:T(8,128)(2,1)S(1)}, u32[]{:S(2)}, u32[]{:S(2)}) collective-permute-start(bf16[1,32,1280]{2,1,0:T(8,128)(2,1)S(1)} %copy.97), channel_id=1, source_target_pairs={{0,1},{1,0},{2,3},{3,2},{4,5},{5,4},{6,7},{7,6},{8,9},{9,8},{10,11... | collective-permute-start | bytes 245768 | tf_op jit(solution)/shard_map/ppermute | solution.py:18
  91.3 2.2 slice-start
  91.6 2.9 %slice-start.1 = ((s8[7372800]{0:T(1024)(128)(4,1)}), s8[3178496]{0:T(1024)(128)(4,1)S(1)}, s32[]{:S(2)}) async-start(s8[7372800]{0:T(1024)(128)(4,1)} %bitcast.120), calls=%async_computation.5 | async-start | bytes 6356992
  91.8 2.7 copy-start.8
  94.5 10.0 %copy-start.3 = (f32[320]{0:T(512)S(1)}, f32[320]{0:T(512)}, u32[]{:S(2)}) copy-start(f32[320]{0:T(512)} %param.17) | copy-start | bytes 3844
  102.8 1.4 collective-permute-start.2
  106.8 119.2 %all-gather.9.cloned.1.call-start = ((), (), s32[]{:S(2)}) async-start(), calls=%async_computation.2 | async-start | bytes 1638400 | tf_op jit(solution)/shard_map/all_gather | solution.py:110
  171.6 6.1 %collective-permute-start.3 = (bf16[1,32,1280]{2,1,0:T(8,128)(2,1)S(1)}, bf16[1,32,1280]{2,1,0:T(8,128)(2,1)S(1)}, u32[]{:S(2)}, u32[]{:S(2)}) collective-permute-start(bf16[1,32,1280]{2,1,0:T(8,128)(2,1)S(1)} %copy.108), channel_id=1, source_target_pairs={{0,1},{1,0},{2,3},{3,2},{4,5},{5,4},{6,7},{7,6},{8,9},{9,8},{10,11... | collective-permute-start | bytes 245768 | tf_op jit(solution)/shard_map/ppermute | solution.py:18
  182.4 2.2 slice-start.2
  182.7 2.9 %slice-start.3 = ((s8[7372800]{0:T(1024)(128)(4,1)}), s8[3178496]{0:T(1024)(128)(4,1)S(1)}, s32[]{:S(2)}) async-start(s8[7372800]{0:T(1024)(128)(4,1)} %bitcast.122), calls=%async_computation.7 | async-start | bytes 6356992
  185.6 8.0 %copy-start.1 = (bf16[16,32,320]{2,1,0:T(8,128)(2,1)S(1)}, bf16[16,32,320]{2,1,0:T(8,128)(2,1)}, u32[]{:S(2)}) copy-start(bf16[16,32,320]{2,1,0:T(8,128)(2,1)} %param.12) | copy-start | bytes 983044
  193.4 2.6 copy-start.4
  193.6 32.3 %copy-start.5 = (bf16[256,1280]{1,0:T(8,128)(2,1)S(1)}, bf16[256,1280]{1,0:T(8,128)(2,1)}, u32[]{:S(2)}) copy-start(bf16[256,1280]{1,0:T(8,128)(2,1)} %param.22) | copy-start | bytes 1966084
  193.6 32.3 %copy-start.6 = (bf16[256,1280]{1,0:T(8,128)(2,1)S(1)}, bf16[256,1280]{1,0:T(8,128)(2,1)}, u32[]{:S(2)}) copy-start(bf16[256,1280]{1,0:T(8,128)(2,1)} %param.21) | copy-start | bytes 1966084
  194.3 1.4 collective-permute-start.4
  197.1 71.5 %all-gather.11.cloned.1.call-start = ((), (), s32[]{:S(2)}) async-start(), calls=%async_computation.3 | async-start | bytes 1310720 | tf_op jit(solution)/shard_map/all_gather | solution.py:129
  228.8 2.0 collective-permute-start.5
Sparse Core Ops, SparseCore 0:
  13.2 63.8 all-gather.4
  106.9 61.2 all-gather.6
  197.2 28.6 all-gather.8
  242.1 26.4 all-gather.10
where the time goes:
time: 278 us
  waiting for transfers between devices  183 us (66%)
  local copies, waits for them, and re-layouts  32 us (12%)
  matrix products  30.8 us (11%)
  other arithmetic  15.9 us (6%)
  between operations  14.3 us (5%)
    all_gather x2, waiting for transfers between devices, convolve(): full = lax.all_gather(active, 'ch', axis=2, tiled=True)  124 us
    all_gather x1, waiting for transfers between devices, body(): lax.all_gather(normed, 'ch', axis=1, tiled=True)  28.8 us
    all_gather x1, waiting for transfers between devices, body(): lax.all_gather(heads_out, 'ch', axis=1, tiled=True)  26.1 us
    conv_general_dilated x2, matrix products, conv_taps(): lax.conv_general_dilated(padded[None], weight, (1, 1), 'VALID', dimension...  15.6 us
    all_gather x2, local copies, waits for them, and re-layouts, convolve(): full = lax.all_gather(active, 'ch', axis=2, tiled=True)  12 us
    select_n x2, other arithmetic, facing_row(): return jnp.where(upper_half, field[-1:], field[:1])  6.06 us
  transfers between devices with their start and end apart: 10, of which 8 were waited for; matrix products, arithmetic and copies ran while one was open for 5% of the time, Pallas kernels for 0%

commit v1 on v0

--- a/solution.py
+++ b/solution.py
@@ -126,7 +126,7 @@
     heads_out = jnp.einsum("hqk,khd->qhd", weights, value_heads, preferred_element_type=jnp.float32)
     heads_out = heads_out.astype(jnp.bfloat16).reshape(tokens, inner)
     weight_cols = w_out
-    projected = right_product(lax.all_gather(heads_out, "ch", axis=1, tiled=True), weight_cols)
+    projected = right_product(jnp.concatenate(lax.all_gather(heads_out, "ch"), axis=1), weight_cols)
     total = hidden_b.reshape(tokens, local_ch) + projected
     return total.reshape(rows, width, local_ch).astype(jnp.bfloat16)
 

time: 278 us -> 279 us (level)
  no operation moved by 1% of the time
where the time goes in v1:
time: 279 us; the launch traced here: 278 us
  waiting for transfers between devices  183 us (66%)
  local copies, waits for them, and re-layouts  34.4 us (12%)
  matrix products  28.8 us (10%)
  other arithmetic  15.9 us (6%)
  between operations  14.3 us (5%)
    all_gather x2, waiting for transfers between devices, convolve(): full = lax.all_gather(active, 'ch', axis=2, tiled=True)  124 us
    all_gather x1, waiting for transfers between devices, body(): lax.all_gather(normed, 'ch', axis=1, tiled=True)  28.8 us
    all_gather x1, waiting for transfers between devices, body(): lax.all_gather(heads_out, 'ch')  26.1 us
    conv_general_dilated x2, matrix products, conv_taps(): lax.conv_general_dilated(padded[None], weight, (1, 1), 'VALID', dimension...  15.6 us
    all_gather x2, local copies, waits for them, and re-layouts, convolve(): full = lax.all_gather(active, 'ch', axis=2, tiled=True)  12 us
    select_n x2, other arithmetic, facing_row(): return jnp.where(upper_half, field[-1:], field[:1])  6.06 us
  transfers between devices with their start and end apart: 10, of which 8 were waited for; matrix products, arithmetic and copies ran while one was open for 5% of the time, Pallas kernels for 0%

profile of v1, /device:TPU:0, one launch (start us, length us, event | category | flops | bytes accessed | tf_op | source)
XLA Modules:
  0.0 278.2 jit_solution(15692118238806772615)
XLA Ops:
  6.5 1.3 convert_reduce_fusion
  9.9 1.3 fusion.55
  11.2 1.8 copy.120
  14.7 62.4 %all-gather.5.cloned.1.call-done = bf16[16,32,1280]{1,0,2:T(8,128)(2,1)} async-done(((bf16[16,32,320]{1,0,2:T(8,128)(2,1)}), bf16[16,32,1280]{1,0,2:T(8,128)(2,1)}) %all-gather.5.cloned.1.call-update) | async-done | bytes 1310736 | tf_op jit(solution)/shard_map/all_gather | solution.py:88
  77.1 3.0 %broadcast_select_fusion.5 = bf16[1,32,1280]{1,0,2:T(2,128)(2,1)S(1)} fusion(pred[]{:T(512)S(6)} %eq.11, bf16[16,32,1280]{1,0,2:T(8,128)(2,1)} %all-gather.5.cloned.1.call-done), kind=kLoop, calls=%fused_computation.48 | loop fusion | flops 40960 | bytes 245761 | tf_op jit(solution)/shard_map/jit(_where)/select_n | solution.py:79
  80.6 6.0 %copy.125 = bf16[16,32,1280]{2,1,0:T(8,128)(2,1)S(1)} copy(bf16[16,32,1280]{1,0,2:T(8,128)(2,1)} %all-gather.5.cloned.1.call-done) | data formatting | bytes 2621440 | tf_op jit(solution)/shard_map/all_gather | solution.py:88
  87.1 1.9 broadcast_select_fusion.4
  89.0 1.3 copy.124
  92.3 1.1 slice-done
  94.5 7.8 %select_reduce_fusion.1 = (f32[320]{0:T(512)S(1)}, f32[320]{0:T(512)S(1)}, f32[16,8,5,320]{3,1,2,0:T(8,128)S(1)}) fusion(f32[320]{0:T(512)S(1)} %divide_multiply_fusion, pred[8,5]{0,1:T(8,128)(4,1)S(1)} %copy-done.8, bf16[320,3,3,1280]{3,0,2,1:T(8,128)(2,1)S(1)} %bitcast.125, bf16[18,1,7,2,1280]{4,2,3,0,1:T(8,128)(2,1)S(1)} %slice.69, ...), kind=kOutput, calls=%fused_computation.59 | convolution fusion | flops 4727766016 | bytes 10684200 | tf_op jit(solution)/shard_map/conv_general_dilated | solution.py:28
  104.8 2.0 copy.131
  106.8 61.4 %all-gather.7.cloned.1.call-done = bf16[16,32,1280]{1,0,2:T(8,128)(2,1)} async-done(((bf16[16,32,320]{1,0,2:T(8,128)(2,1)}), bf16[16,32,1280]{1,0,2:T(8,128)(2,1)}) %all-gather.7.cloned.1.call-update) | async-done | bytes 1310736 | tf_op jit(solution)/shard_map/all_gather | solution.py:88
  168.2 3.0 %broadcast_select_fusion.2 = bf16[1,32,1280]{1,0,2:T(2,128)(2,1)S(1)} fusion(pred[]{:T(512)S(6)} %eq.11, bf16[16,32,1280]{1,0,2:T(8,128)(2,1)} %all-gather.7.cloned.1.call-done), kind=kLoop, calls=%fused_computation.45 | loop fusion | flops 40960 | bytes 245761 | tf_op jit(solution)/shard_map/jit(_where)/select_n | solution.py:79
  171.7 6.0 %copy.136 = bf16[16,32,1280]{2,1,0:T(8,128)(2,1)S(1)} copy(bf16[16,32,1280]{1,0,2:T(8,128)(2,1)} %all-gather.7.cloned.1.call-done) | data formatting | bytes 2621440 | tf_op jit(solution)/shard_map/all_gather | solution.py:88
  178.2 1.9 broadcast_select_fusion.1
  180.1 1.3 copy.135
  185.6 7.8 %fusion.35 = f32[16,8,5,320]{3,1,2,0:T(8,128)S(1)} fusion(bf16[320,3,3,1280]{3,0,2,1:T(8,128)(2,1)S(1)} %bitcast.127, bf16[18,1,7,2,1280]{4,2,3,0,1:T(8,128)(2,1)S(1)} %slice.73, bf16[18,1,8,5,1280]{4,2,3,0,1:T(8,128)(2,1)S(1)} %copy.140, pred[8,5]{0,1:T(8,128)(4,1)S(1)} %copy-done.8), kind=kOutput, calls=%fused_computation.49 | convolution fusion | flops 4726538240 | bytes 10680360 | tf_op jit(solution)/shard_map/conv_general_dilated | solution.py:28
  197.2 28.8 %all-gather.9.cloned.1.call-done = bf16[512,1280]{0,1:T(8,128)(2,1)} async-done(((bf16[512,320]{0,1:T(8,128)(2,1)}), bf16[512,1280]{0,1:T(8,128)(2,1)}) %all-gather.9.cloned.1.call-update) | async-done | bytes 1310736 | tf_op jit(solution)/shard_map/all_gather | solution.py:110
  225.9 2.7 fusion.32
  229.0 1.7 collective-permute-done.5
  231.3 5.0 %fusion.81 = (f32[4,512]{1,0:T(4,128)S(1)}, f32[4,512,1024]{2,1,0:T(8,128)}) fusion(bf16[512,4,64]{0,2,1:T(8,128)(2,1)S(1)} %bitcast.110, bf16[1024,4,64]{0,2,1:T(8,128)(2,1)S(1)} %bitcast.108), kind=kOutput, calls=%fused_computation.118 | convolution fusion | flops 274727936 | bytes 9183232 | tf_op jit(solution)/shard_map/sub | solution.py:124
  236.4 4.8 %fusion.44 = bf16[4,64,512]{2,1,0:T(8,128)(2,1)S(1)} fusion(bf16[1024,4,64]{0,2,1:T(8,128)(2,1)S(1)} %bitcast.109, f32[4,512,1024]{2,1,0:T(8,128)} %get-tuple-element.23, f32[4,512]{1,0:T(4,128)S(1)} %get-tuple-element.22), kind=kOutput, calls=%fused_computation.55 | convolution fusion | flops 272760832 | bytes 9183232 | tf_op jit(solution)/shard_map/hqk,khd->qhd/dot_general | solution.py:126
  242.6 26.1 %all-gather.11.cloned.1.call-done = bf16[4,512,256]{2,1,0:T(8,128)(2,1)} async-done(((bf16[1,512,256]{2,1,0:T(8,128)(2,1)}), bf16[4,512,256]{2,1,0:T(8,128)(2,1)}) %all-gather.11.cloned.1.call-update) | async-done | bytes 1048592 | tf_op jit(solution)/shard_map/all_gather | solution.py:129
  268.7 1.5 copy.149
  (123 shorter events, 22.1 us)
Async XLA Ops:
  6.5 263.7 %copy-start = (bf16[320,1024]{1,0:T(8,128)(2,1)S(1)}, bf16[320,1024]{1,0:T(8,128)(2,1)}, u32[]{:S(2)}) copy-start(bf16[320,1024]{1,0:T(8,128)(2,1)} %param.23) | copy-start | bytes 1966084
  6.5 6.6 %copy-start.7 = (s32[4]{0:T(128)S(1)}, s32[4]{0:T(128)}, u32[]{:S(2)}) copy-start(s32[4]{0:T(128)} %param.13) | copy-start | bytes 52
  6.5 8.0 %copy-start.2 = (bf16[320,320]{1,0:T(8,128)(2,1)S(1)}, bf16[320,320]{1,0:T(8,128)(2,1)}, u32[]{:S(2)}) copy-start(bf16[320,320]{1,0:T(8,128)(2,1)} %param.16) | copy-start | bytes 614404
  6.5 70.5 %all-gather.5.cloned.1.call-start = ((), (), s32[]{:S(2)}) async-start(), calls=%async_computation | async-start | bytes 6553600 | tf_op jit(solution)/shard_map/all_gather | solution.py:88
  8.2 1.4 collective-permute-start
  13.0 155.2 %all-gather.7.cloned.1.call-start = ((), (), s32[]{:S(2)}) async-start(), calls=%async_computation.1 | async-start | bytes 6553600 | tf_op jit(solution)/shard_map/all_gather | solution.py:88
  80.5 6.1 %collective-permute-start.1 = (bf16[1,32,1280]{2,1,0:T(8,128)(2,1)S(1)}, bf16[1,32,1280]{2,1,0:T(8,128)(2,1)S(1)}, u32[]{:S(2)}, u32[]{:S(2)}) collective-permute-start(bf16[1,32,1280]{2,1,0:T(8,128)(2,1)S(1)} %copy.121), channel_id=1, source_target_pairs={{0,1},{1,0},{2,3},{3,2},{4,5},{5,4},{6,7},{7,6},{8,9},{9,8},{10,11... | collective-permute-start | bytes 245768 | tf_op jit(solution)/shard_map/ppermute | solution.py:18
  91.3 2.2 slice-start
  91.6 2.9 %slice-start.1 = ((s8[7372800]{0:T(1024)(128)(4,1)}), s8[3178496]{0:T(1024)(128)(4,1)S(1)}, s32[]{:S(2)}) async-start(s8[7372800]{0:T(1024)(128)(4,1)} %bitcast.124), calls=%async_computation.5 | async-start | bytes 6356992
  91.8 2.7 copy-start.8
  94.5 10.0 %copy-start.3 = (f32[320]{0:T(512)S(1)}, f32[320]{0:T(512)}, u32[]{:S(2)}) copy-start(f32[320]{0:T(512)} %param.17) | copy-start | bytes 3844
  102.8 1.4 collective-permute-start.2
  106.8 119.2 %all-gather.9.cloned.1.call-start = ((), (), s32[]{:S(2)}) async-start(), calls=%async_computation.2 | async-start | bytes 1638400 | tf_op jit(solution)/shard_map/all_gather | solution.py:110
  171.6 6.1 %collective-permute-start.3 = (bf16[1,32,1280]{2,1,0:T(8,128)(2,1)S(1)}, bf16[1,32,1280]{2,1,0:T(8,128)(2,1)S(1)}, u32[]{:S(2)}, u32[]{:S(2)}) collective-permute-start(bf16[1,32,1280]{2,1,0:T(8,128)(2,1)S(1)} %copy.132), channel_id=1, source_target_pairs={{0,1},{1,0},{2,3},{3,2},{4,5},{5,4},{6,7},{7,6},{8,9},{9,8},{10,11... | collective-permute-start | bytes 245768 | tf_op jit(solution)/shard_map/ppermute | solution.py:18
  182.4 2.2 slice-start.2
  182.7 2.9 %slice-start.3 = ((s8[7372800]{0:T(1024)(128)(4,1)}), s8[3178496]{0:T(1024)(128)(4,1)S(1)}, s32[]{:S(2)}) async-start(s8[7372800]{0:T(1024)(128)(4,1)} %bitcast.126), calls=%async_computation.7 | async-start | bytes 6356992
  185.6 8.0 %copy-start.1 = (bf16[16,32,320]{2,1,0:T(8,128)(2,1)S(1)}, bf16[16,32,320]{2,1,0:T(8,128)(2,1)}, u32[]{:S(2)}) copy-start(bf16[16,32,320]{2,1,0:T(8,128)(2,1)} %param.12) | copy-start | bytes 983044
  193.4 2.6 copy-start.4
  193.6 32.3 %copy-start.5 = (bf16[256,1280]{1,0:T(8,128)(2,1)S(1)}, bf16[256,1280]{1,0:T(8,128)(2,1)}, u32[]{:S(2)}) copy-start(bf16[256,1280]{1,0:T(8,128)(2,1)} %param.22) | copy-start | bytes 1966084
  193.6 32.3 %copy-start.6 = (bf16[256,1280]{1,0:T(8,128)(2,1)S(1)}, bf16[256,1280]{1,0:T(8,128)(2,1)}, u32[]{:S(2)}) copy-start(bf16[256,1280]{1,0:T(8,128)(2,1)} %param.21) | copy-start | bytes 1966084
  194.3 1.4 collective-permute-start.4
  197.1 71.6 %all-gather.11.cloned.1.call-start = ((), (), s32[]{:S(2)}) async-start(), calls=%async_computation.3 | async-start | bytes 1310720 | tf_op jit(solution)/shard_map/all_gather | solution.py:129
  228.8 2.0 collective-permute-start.5
Sparse Core Ops, SparseCore 0:
  13.2 63.8 all-gather.4
  106.9 61.2 all-gather.6
  197.2 28.6 all-gather.8
  242.2 26.4 all-gather.10
